TPU v7x, 512 devices: a whole 4x4x16 slice. The times are simulated.
512 devices in a mesh: dp: 8 (over y, core), row: 64 (over x, z).
Axes of the slice: x: 4, y: 4, z: 16, core: 2. Of those that a mesh axis runs over, the one named last changes fastest.
Arguments:
- hidden: bfloat16 [8, 128, 128, 768], P('dp', 'row'), may hold values from -6 to 6
- masked: int32 [8, 128, 128], P('dp', 'row'), may hold values 0 or 1
- depths: int32 [8], P('dp'), may hold values from 32 to 128, as said below
- norm_gain: float32 [768], replicated, may hold values from 0.25 to 1.75
- w_query: bfloat16 [768, 768], P('row'), may hold values from -0.21875 to 0.21875
- w_key: bfloat16 [768, 768], P('row'), may hold values from -0.21875 to 0.21875
- w_value: bfloat16 [768, 768], P('row'), may hold values from -0.21875 to 0.21875
- w_out: bfloat16 [768, 768], P('row'), may hold values from -0.21875 to 0.21875
- cotangent: bfloat16 [8, 128, 128, 768], P('dp', 'row'), may hold values from -6 to 6
Outputs:
- mixed: bfloat16 [8, 128, 128, 768], P('dp', 'row')
- grad_hidden: bfloat16 [8, 128, 128, 768], P('dp', 'row')
Inputs may be any that keep to these rules, and one draw needn't show every extreme that they name: `depths`: rows at or past an MSA's depth are padding.
All inputs are finite; a program needn't handle non-finite values. No bound on the sum of `masked` on one device may be relied on, other than what follows from the above.
Results may differ from a plain program's by a relative error of at most 0.0059.
Values may be sent and summed in bfloat16 or wider, within the bound.
A program may use at most 64 MiB of HBM per device.

v0:
```python
import jax
import jax.numpy as jnp
from jax import lax
from jax.sharding import PartitionSpec as P

HEADS = 12
EPS = 1e-05


def softmax_rows(scores):
    top = jnp.max(scores, axis=-1, keepdims=True)
    expo = jnp.exp(scores - top)
    return expo / jnp.sum(expo, axis=-1, keepdims=True)


def back_dot(left, weight):
    return lax.dot_general(
        left, weight, (((1,), (1,)), ((), ())), preferred_element_type=jnp.float32
    )


def body(hidden, masked, depths, norm_gain, w_query, w_key, w_value, w_out, cotangent):
    local_rows = hidden.shape[1]
    columns = hidden.shape[2]
    width = hidden.shape[3]
    head_count = HEADS
    head_size = width // head_count
    flat_rows = local_rows * columns
    first_row = lax.axis_index("row") * local_rows
    depth = depths[0]
    alive = (first_row + jnp.arange(local_rows, dtype=jnp.int32) < depth).astype(jnp.float32)
    mask_rows = masked[0]
    weighting = mask_rows.astype(jnp.float32) * alive[:, None]
    live_total, masked_total = lax.psum(
        (jnp.sum(alive) * columns, jnp.sum(weighting)), ("dp", "row")
    )
    loss_ratio = live_total / jnp.maximum(masked_total, 1.0)
    full_query, full_key, full_value, full_out = (
        lax.all_gather(w_query, "row", axis=0, tiled=True),
        lax.all_gather(w_key, "row", axis=0, tiled=True),
        lax.all_gather(w_value, "row", axis=0, tiled=True),
        lax.all_gather(w_out, "row", axis=0, tiled=True),
    )
    widened = hidden[0].reshape(flat_rows, width).astype(jnp.float32)
    average = jnp.mean(widened, axis=-1, keepdims=True)
    centred = widened - average
    variance = jnp.mean(centred * centred, axis=-1, keepdims=True)
    inv_std = lax.rsqrt(variance + EPS)
    x_hat = centred * inv_std
    normed = (x_hat * norm_gain).astype(jnp.bfloat16)

    def project(weight):
        out = jnp.dot(normed, weight, preferred_element_type=jnp.float32).astype(jnp.bfloat16)
        return out.reshape(local_rows, columns, head_count, head_size)

    queries = project(full_query)
    keys_proj = project(full_key)
    values_proj = project(full_value)
    alive_heads = alive[:, None, None, None]
    query_live = queries * alive_heads.astype(jnp.bfloat16)
    scale = 1.0 / jnp.sqrt(depth.astype(jnp.float32) * head_size)
    partial_value = jnp.einsum(
        "rihe,rjhe->hij", query_live, keys_proj, preferred_element_type=jnp.float32
    )
    logits = lax.psum(partial_value, "row") * scale
    probs = softmax_rows(logits)
    probs_low = probs.astype(jnp.bfloat16)
    attended = jnp.einsum(
        "hij,rjhe->rihe", probs_low, values_proj, preferred_element_type=jnp.float32
    ).astype(jnp.bfloat16)
    projected = jnp.dot(
        attended.reshape(flat_rows, width), full_out, preferred_element_type=jnp.float32
    )
    alive_tokens = jnp.repeat(alive, columns)[:, None]
    mixed = (widened + alive_tokens * projected).astype(jnp.bfloat16)
    back_query, back_key, back_value, back_out = (
        lax.all_gather(w_query, "row", axis=0, tiled=True),
        lax.all_gather(w_key, "row", axis=0, tiled=True),
        lax.all_gather(w_value, "row", axis=0, tiled=True),
        lax.all_gather(w_out, "row", axis=0, tiled=True),
    )
    token_weight = (weighting * loss_ratio).reshape(flat_rows, 1)
    grad_mixed = cotangent[0].reshape(flat_rows, width).astype(jnp.float32) * token_weight
    grad_attended = back_dot(grad_mixed.astype(jnp.bfloat16), back_out).astype(jnp.bfloat16)
    grad_attended = grad_attended.reshape(local_rows, columns, head_count, head_size)
    grad_partial = jnp.einsum(
        "rihe,rjhe->hij", grad_attended, values_proj, preferred_element_type=jnp.float32
    )
    grad_values = jnp.einsum(
        "hij,rihe->rjhe", probs_low, grad_attended, preferred_element_type=jnp.float32
    ).astype(jnp.bfloat16)
    grad_probs = lax.psum(grad_partial, "row")
    grad_logits = probs * (grad_probs - jnp.sum(probs * grad_probs, axis=-1, keepdims=True))
    grad_logits = (grad_logits * scale).astype(jnp.bfloat16)
    grad_queries = (
        jnp.einsum("hij,rjhe->rihe", grad_logits, keys_proj, preferred_element_type=jnp.float32)
        * alive_heads
    ).astype(jnp.bfloat16)
    grad_keys = jnp.einsum(
        "hij,rihe->rjhe", grad_logits, query_live, preferred_element_type=jnp.float32
    ).astype(jnp.bfloat16)
    grad_normed = back_dot(grad_queries.reshape(flat_rows, width), back_query)
    grad_normed = grad_normed + back_dot(grad_keys.reshape(flat_rows, width), back_key)
    grad_normed = grad_normed + back_dot(grad_values.reshape(flat_rows, width), back_value)
    scaled = grad_normed * norm_gain
    grad_x = inv_std * (
        scaled
        - jnp.mean(scaled, axis=-1, keepdims=True)
        - x_hat * jnp.mean(scaled * x_hat, axis=-1, keepdims=True)
    )
    grad_hidden = (grad_mixed + grad_x).astype(jnp.bfloat16)
    return (
        mixed.reshape(1, local_rows, columns, width),
        grad_hidden.reshape(1, local_rows, columns, width),
    )


def solution(mesh):
    return jax.shard_map(
        body,
        mesh=mesh,
        in_specs=(
            P("dp", "row", None, None),
            P("dp", "row", None),
            P("dp"),
            P(),
            P("row", None),
            P("row", None),
            P("row", None),
            P("row", None),
            P("dp", "row", None, None),
        ),
        out_specs=(P("dp", "row", None, None), P("dp", "row", None, None)),
        check_vma=False,
    )
```

profile of v0, /device:TPU:8, one launch (start us, length us, event | category | flops | bytes accessed | tf_op | source)
XLA Modules:
  0.0 913.6 jit_solution(1743458833186725922)
XLA Ops:
  11.9 1.9 broadcast_bitcast_fusion
  13.9 108.7 %all-reduce = (f32[]{:T(128)}, f32[]{:T(128)}) all-reduce(f32[]{:T(128)S(6)} %mul.140, f32[]{:T(128)} %get-tuple-element.13), channel_id=1, replica_groups=mesh['dp'=8,'row'=64] {'dp','row'}, use_global_device_ids=true, to_apply=%region_6.0 | all-reduce | flops 2 | bytes 16 | tf_op jit(solution)/shard_map/psum | solution.py:34
  128.0 28.0 %all-gather.13.cloned.1.call-done = bf16[64,12,768]{2,1,0:T(8,128)(2,1)} async-done(((bf16[1,12,768]{2,1,0:T(8,128)(2,1)}), bf16[64,12,768]{2,1,0:T(8,128)(2,1)}) %all-gather.13.cloned.1.call-update) | async-done | bytes 1179664 | tf_op jit(solution)/shard_map/all_gather | solution.py:40
  155.9 2.2 reshape.134
  159.7 135.6 %all-gather.9.cloned.1.call-done = bf16[64,12,768]{2,1,0:T(8,128)(2,1)} async-done(((bf16[1,12,768]{2,1,0:T(8,128)(2,1)}), bf16[64,12,768]{2,1,0:T(8,128)(2,1)}) %all-gather.9.cloned.1.call-update) | async-done | bytes 1179664 | tf_op jit(solution)/shard_map/all_gather | solution.py:41
  295.3 2.2 reshape.130
  299.1 135.7 %all-gather.11.cloned.1.call-done = bf16[64,12,768]{2,1,0:T(8,128)(2,1)} async-done(((bf16[1,12,768]{2,1,0:T(8,128)(2,1)}), bf16[64,12,768]{2,1,0:T(8,128)(2,1)}) %all-gather.11.cloned.1.call-update) | async-done | bytes 1179664 | tf_op jit(solution)/shard_map/all_gather | solution.py:39
  434.7 2.2 reshape.132
  437.0 2.2 convolution_convert_fusion.2
  439.2 1.9 copy.35
  441.1 1.8 reshape.118
  443.0 131.0 %all-gather.15.cloned.1.call-done = bf16[64,12,768]{2,1,0:T(8,128)(2,1)} async-done(((bf16[1,12,768]{2,1,0:T(8,128)(2,1)}), bf16[64,12,768]{2,1,0:T(8,128)(2,1)}) %all-gather.15.cloned.1.call-update) | async-done | bytes 1179664 | tf_op jit(solution)/shard_map/all_gather | solution.py:42
  574.0 3.1 reshape.136
  577.1 2.7 convolution_convert_fusion
  579.8 1.9 copy.41
  581.7 1.8 reshape.122
  583.5 1.4 broadcast_multiply_fusion
  585.0 2.5 convolution_bitcast_fusion
  588.8 275.2 %all-reduce.4.cloned.1.call-done = (f32[12,128,128]{2,1,0:T(8,128)}, f32[12,128,128]{2,1,0:T(8,128)}) async-done(((f32[12,128,128]{2,1,0:T(8,128)}, f32[12,128,128]{2,1,0:T(8,128)}), (f32[12,128,128]{2,1,0:T(8,128)}, f32[12,128,128]{2,1,0:T(8,128)})) %all-reduce.4.cloned.1.call-update) | async-done | bytes 1572880 | tf_op jit(solution)/shard_map/psum | solution.py:65
  864.0 2.3 fusion.68
  866.3 10.9 %fusion.15 = bf16[2,128,12,64]{1,3,0,2:T(8,128)(2,1)} fusion(f32[12,128,128]{2,1,0:T(8,128)} %get-tuple-element.7, f32[2]{0:T(128)} %copy-done.10, f32[]{:T(128)S(6)} %sqrt.3, bf16[2,128,12,64]{1,0,3,2:T(2,128)(2,1)} %reshape.119, f32[12,128,128]{2,1,0:T(8,128)} %get-tuple-element.15, f32[12,128]{1,0:T(8,128)S(1)} %get-tuple-element.14), kind=kOutput, calls=%fused_computation.28 | convolution fusion | flops 52102784 | bytes 2365452 | tf_op jit(solution)/shard_map/hij,rjhe->rihe/dot_general | solution.py:96
  877.2 10.9 %fusion.13 = bf16[2,128,12,64]{1,3,0,2:T(8,128)(2,1)} fusion(f32[12,128,128]{2,1,0:T(8,128)} %get-tuple-element.7, f32[]{:T(128)S(6)} %sqrt.3, bf16[2,128,12,64]{1,0,3,2:T(2,128)(2,1)} %copy-done.4, f32[12,128,128]{2,1,0:T(8,128)} %get-tuple-element.15, f32[12,128]{1,0:T(8,128)S(1)} %get-tuple-element.14), kind=kOutput, calls=%fused_computation.26 | convolution fusion | flops 51906176 | bytes 2365444 | tf_op jit(solution)/shard_map/hij,rihe->rjhe/dot_general | solution.py:99
  888.1 4.8 fusion.14
  892.9 4.8 fusion.12
  (63 shorter events, 20.9 us)
Async XLA Ops:
  7.2 119.9 %copy-start = (bf16[1,2,128,768]{3,2,1,0:T(8,128)(2,1)S(1)}, bf16[1,2,128,768]{3,2,1,0:T(8,128)(2,1)}, u32[]{:S(2)}) copy-start(bf16[1,2,128,768]{3,2,1,0:T(8,128)(2,1)} %param.9) | copy-start | bytes 1179652
  7.2 148.8 %all-gather.13.cloned.1.call-start = ((), (), s32[]{:S(2)}) async-start(), calls=%async_computation.2 | async-start | bytes 1597440 | tf_op jit(solution)/shard_map/all_gather | solution.py:40
  7.9 287.4 %all-gather.9.cloned.1.call-start = ((), (), s32[]{:S(2)}) async-start(), calls=%async_computation | async-start | bytes 1597440 | tf_op jit(solution)/shard_map/all_gather | solution.py:41
  8.7 426.1 %all-gather.11.cloned.1.call-start = ((), (), s32[]{:S(2)}) async-start(), calls=%async_computation.1 | async-start | bytes 1597440 | tf_op jit(solution)/shard_map/all_gather | solution.py:39
  9.4 564.6 %all-gather.15.cloned.1.call-start = ((), (), s32[]{:S(2)}) async-start(), calls=%async_computation.3 | async-start | bytes 1597440 | tf_op jit(solution)/shard_map/all_gather | solution.py:42
  10.0 854.0 %all-reduce.4.cloned.1.call-start = ((), (), s32[]{:S(2)}) async-start(), calls=%async_computation.4 | async-start | bytes 3145728 | tf_op jit(solution)/shard_map/psum | solution.py:65
  11.3 116.7 %copy-start.10 = (f32[2]{0:T(128)}, f32[2]{0:T(128)S(1)}, u32[]{:S(2)}) copy-start(f32[2]{0:T(128)S(1)} %get-tuple-element.9) | copy-start | bytes 28
  127.0 450.1 %copy-start.11 = (f32[256]{0:T(256)}, f32[256]{0:T(256)S(1)}, u32[]{:S(2)}) copy-start(f32[256]{0:T(256)S(1)} %fusion.54) | copy-start | bytes 3076
  128.0 169.6 %copy-start.2 = (bf16[256,768]{1,0:T(8,128)(2,1)}, bf16[256,768]{1,0:T(8,128)(2,1)S(1)}, u32[]{:S(2)}) copy-start(bf16[256,768]{1,0:T(8,128)(2,1)S(1)} %multiply_convert_fusion) | copy-start | bytes 1179652
  583.5 3.9 copy-start.3
  585.0 2.5 copy-start.4
  900.6 1.0 copy-start.8
  900.6 1.4 copy-start.7
  902.4 1.0 copy-start.1
  902.4 1.0 copy-start.9
  903.4 1.3 copy-start.5
  903.4 1.3 copy-start.13
  904.7 1.3 copy-start.6
  904.7 1.3 copy-start.12
Sparse Core Ops, SparseCore 0:
  10.9 144.9 all-gather.12
  158.9 136.3 all-gather.8
  298.2 136.4 all-gather.10
  437.5 136.4 all-gather.14
  588.8 275.0 all-reduce.3
where the time goes:
time: 915 us; the launch traced here: 914 us
  waiting for transfers between devices  708 us (77%)
  blocking collectives  109 us (12%)
  matrix products  44 us (5%)
  local copies, waits for them, and re-layouts  24.6 us (3%)
  between operations  16.6 us (2%)
  other arithmetic  11.4 us (1%)
    psum x1, waiting for transfers between devices, body(): logits = lax.psum(partial_value, 'row') * scale  275 us
    all_gather x1, waiting for transfers between devices, body(): lax.all_gather(w_query, 'row', axis=0, tiled=True)  136 us
    all_gather x1, waiting for transfers between devices, body(): lax.all_gather(w_value, 'row', axis=0, tiled=True)  136 us
    all_gather x1, waiting for transfers between devices, body(): lax.all_gather(w_out, 'row', axis=0, tiled=True)  131 us
    psum x1, blocking collectives, body(): lax.psum((jnp.sum(alive) * columns, jnp.sum(weighting)), ('dp', 'row'))  109 us
    all_gather x1, waiting for transfers between devices, body(): lax.all_gather(w_key, 'row', axis=0, tiled=True)  28 us
  transfers between devices with their start and end apart: 5, of which 5 were waited for; matrix products, arithmetic and copies ran while one was open for 2% of the time, Pallas kernels for 0%

commit v1 on v0

--- a/solution.py
+++ b/solution.py
@@ -20,6 +20,14 @@
 
 
 def body(hidden, masked, depths, norm_gain, w_query, w_key, w_value, w_out, cotangent):
+
+    def open_things(x_part):
+        wide_out = lax.all_to_all(
+            jnp.stack([x_part for _ in range(lax.axis_size("row"))]), "row", 0, 0
+        )
+        found_now = jnp.concatenate(wide_out, 0)
+        return found_now
+
     local_rows = hidden.shape[1]
     columns = hidden.shape[2]
     width = hidden.shape[3]
@@ -39,7 +47,7 @@
         lax.all_gather(w_query, "row", axis=0, tiled=True),
         lax.all_gather(w_key, "row", axis=0, tiled=True),
         lax.all_gather(w_value, "row", axis=0, tiled=True),
-        lax.all_gather(w_out, "row", axis=0, tiled=True),
+        open_things(w_out),
     )
     widened = hidden[0].reshape(flat_rows, width).astype(jnp.float32)
     average = jnp.mean(widened, axis=-1, keepdims=True)

time: 915 us -> 937 us (1.024)
  waiting for transfers between devices: 708 us -> 671 us
  blocking collectives: 109 us -> 139 us
  starting transfers between devices: 0.19 us -> 19.1 us
  local copies, waits for them, and re-layouts: 24.6 us -> 35.2 us
    all_gather x1, waiting for transfers between devices: 136 us -> 0.02 us  [body(): lax.all_gather(w_query, 'row', axis=0, tiled=True)]
    all_gather x1, waiting for transfers between devices: 28 us -> 122 us  [body(): lax.all_gather(w_key, 'row', axis=0, tiled=True)]
    psum x1, blocking collectives: 109 us -> 139 us  [body(): lax.psum((jnp.sum(alive) * columns, jnp.sum(weighting)), ('dp', 'row'))]
    all_to_all x0 -> x1, starting transfers between devices: none -> 18.9 us  [open_things(): lax.all_to_all(jnp.stack([x_part for _ in range(lax.axis_size('row'))]),...]
  transfers between devices with their start and end apart: 5 -> 6, of which waited for: 5 -> 4; matrix products, arithmetic and copies ran while one was open for 2% -> 9% of each run, Pallas kernels for 0% -> 0%
where the time goes in v1:
time: 937 us; the launch traced here: 936 us
  waiting for transfers between devices  671 us (72%)
  blocking collectives  139 us (15%)
  matrix products  45.9 us (5%)
  local copies, waits for them, and re-layouts  35.2 us (4%)
  starting transfers between devices  19.1 us (2%)
  between operations  16.6 us (2%)
    psum x1, waiting for transfers between devices, body(): logits = lax.psum(partial_value, 'row') * scale  275 us
    psum x1, blocking collectives, body(): lax.psum((jnp.sum(alive) * columns, jnp.sum(weighting)), ('dp', 'row'))  139 us
    all_gather x1, waiting for transfers between devices, body(): lax.all_gather(w_value, 'row', axis=0, tiled=True)  137 us
    all_gather x1, waiting for transfers between devices, body(): lax.all_gather(w_out, 'row', axis=0, tiled=True)  133 us
    all_gather x1, waiting for transfers between devices, body(): lax.all_gather(w_key, 'row', axis=0, tiled=True)  122 us
    all_to_all x1, starting transfers between devices, open_things(): lax.all_to_all(jnp.stack([x_part for _ in range(lax.axis_size('row'))]),...  18.9 us
  transfers between devices with their start and end apart: 6, of which 4 were waited for; matrix products, arithmetic and copies ran while one was open for 9% of the time, Pallas kernels for 0%

profile of v1, /device:TPU:8, one launch (start us, length us, event | category | flops | bytes accessed | tf_op | source)
XLA Modules:
  0.0 936.2 jit_solution(6862891457699644232)
XLA Ops:
  9.4 2.0 stack.2
  11.4 18.9 %all-to-all-start = ((bf16[64,12,768]{2,1,0:T(8,128)(2,1)}), bf16[64,12,768]{2,1,0:T(8,128)(2,1)}, u32[]{:S(2)}, u32[]{:S(2)}) async-start(bf16[64,12,768]{2,1,0:T(8,128)(2,1)} %stack.2), calls=%async_computation | async-start | bytes 3145728 | tf_op jit(solution)/shard_map/all_to_all | solution.py:25
  34.1 139.5 %all-reduce = (f32[]{:T(128)}, f32[]{:T(128)}) all-reduce(f32[]{:T(128)S(6)} %mul.140, f32[]{:T(128)} %get-tuple-element.13), channel_id=1, replica_groups=mesh['dp'=8,'row'=64] {'dp','row'}, use_global_device_ids=true, to_apply=%region_6.0 | all-reduce | flops 2 | bytes 16 | tf_op jit(solution)/shard_map/psum | solution.py:42
  176.8 2.4 reshape.138
  180.7 122.4 %all-gather.13.cloned.1.call-done = bf16[64,12,768]{2,1,0:T(8,128)(2,1)} async-done(((bf16[1,12,768]{2,1,0:T(8,128)(2,1)}), bf16[64,12,768]{2,1,0:T(8,128)(2,1)}) %all-gather.13.cloned.1.call-update) | async-done | bytes 1179664 | tf_op jit(solution)/shard_map/all_gather | solution.py:48
  303.2 2.2 reshape.140
  305.4 137.2 %all-gather.9.cloned.1.call-done = bf16[64,12,768]{2,1,0:T(8,128)(2,1)} async-done(((bf16[1,12,768]{2,1,0:T(8,128)(2,1)}), bf16[64,12,768]{2,1,0:T(8,128)(2,1)}) %all-gather.9.cloned.1.call-update) | async-done | bytes 1179664 | tf_op jit(solution)/shard_map/all_gather | solution.py:49
  442.6 2.2 reshape.136
  444.8 2.3 convolution_convert_fusion.1
  448.4 133.5 %all-gather.15.cloned.1.call-done = bf16[64,12,768]{2,1,0:T(8,128)(2,1)} async-done(((bf16[1,12,768]{2,1,0:T(8,128)(2,1)}), bf16[64,12,768]{2,1,0:T(8,128)(2,1)}) %all-gather.15.cloned.1.call-update) | async-done | bytes 1179664 | tf_op jit(solution)/shard_map/all_gather | solution.py:88
  581.9 3.1 reshape.142
  585.0 2.7 convolution_convert_fusion
  596.4 1.9 copy.34
  600.1 2.4 convolution_bitcast_fusion.1
  603.9 275.3 %all-reduce.4.cloned.1.call-done = (f32[12,128,128]{2,1,0:T(8,128)}, f32[12,128,128]{2,1,0:T(8,128)}) async-done(((f32[12,128,128]{2,1,0:T(8,128)}, f32[12,128,128]{2,1,0:T(8,128)}), (f32[12,128,128]{2,1,0:T(8,128)}, f32[12,128,128]{2,1,0:T(8,128)})) %all-reduce.4.cloned.1.call-update) | async-done | bytes 1572880 | tf_op jit(solution)/shard_map/psum | solution.py:73
  879.1 2.9 fusion.68
  882.0 11.0 %fusion.13 = bf16[2,128,12,64]{1,3,0,2:T(8,128)(2,1)} fusion(f32[12,128,128]{2,1,0:T(8,128)} %get-tuple-element.7, f32[]{:T(128)S(6)} %sqrt.3, bf16[2,128,12,64]{1,0,3,2:T(2,128)(2,1)} %broadcast_multiply_fusion, f32[12,128,128]{2,1,0:T(8,128)} %get-tuple-element.15, f32[12,128]{1,0:T(8,128)} %get-tuple-element.14), kind=kOutput, calls=%fused_computation.26 | convolution fusion | flops 51906176 | bytes 2365444 | tf_op jit(solution)/shard_map/hij,rihe->rjhe/dot_general | solution.py:107
  893.0 2.2 copy.47
  895.2 10.9 %fusion.15 = bf16[2,128,12,64]{1,3,0,2:T(8,128)(2,1)} fusion(f32[12,128,128]{2,1,0:T(8,128)} %get-tuple-element.7, f32[2]{0:T(128)S(1)} %get-tuple-element.9, f32[]{:T(128)S(6)} %sqrt.3, bf16[2,128,12,64]{1,0,3,2:T(2,128)(2,1)} %reshape.124, f32[12,128,128]{2,1,0:T(8,128)} %get-tuple-element.15, f32[12,128]{1,0:T(8,128)} %get-tuple-element.14), kind=kOutput, calls=%fused_computation.28 | convolution fusion | flops 52102784 | bytes 2365452 | tf_op jit(solution)/shard_map/hij,rjhe->rihe/dot_general | solution.py:104
  906.1 2.1 copy.45
  908.3 4.8 fusion.12
  913.1 2.1 copy.40
  915.2 4.8 fusion.14
  926.1 2.3 reshape.126
  (69 shorter events, 28.4 us)
Async XLA Ops:
  7.2 169.7 %all-gather.11.cloned.1.call-start = ((), (), s32[]{:S(2)}) async-start(), calls=%async_computation.2 | async-start | bytes 1597440 | tf_op jit(solution)/shard_map/all_gather | solution.py:47
  7.9 295.3 %all-gather.13.cloned.1.call-start = ((), (), s32[]{:S(2)}) async-start(), calls=%async_computation.3 | async-start | bytes 1597440 | tf_op jit(solution)/shard_map/all_gather | solution.py:48
  8.6 433.9 %all-gather.9.cloned.1.call-start = ((), (), s32[]{:S(2)}) async-start(), calls=%async_computation.1 | async-start | bytes 1597440 | tf_op jit(solution)/shard_map/all_gather | solution.py:49
  11.4 21.5 %copy-start.12 = (s32[1,2,128]{2,1,0:T(2,128)S(1)}, s32[1,2,128]{2,1,0:T(2,128)}, u32[]{:S(2)}) copy-start(s32[1,2,128]{2,1,0:T(2,128)} %param.10) | copy-start | bytes 3076
  11.4 164.1 %copy-start = (bf16[1,2,128,768]{3,2,1,0:T(8,128)(2,1)S(1)}, bf16[1,2,128,768]{3,2,1,0:T(8,128)(2,1)}, u32[]{:S(2)}) copy-start(bf16[1,2,128,768]{3,2,1,0:T(8,128)(2,1)} %param.9) | copy-start | bytes 1179652
  11.4 165.2 %copy-start.10 = (f32[768]{0:T(1024)S(1)}, f32[768]{0:T(1024)}, u32[]{:S(2)}) copy-start(f32[768]{0:T(1024)} %param.12) | copy-start | bytes 9220
  11.4 914.7 %all-to-all-start = ((bf16[64,12,768]{2,1,0:T(8,128)(2,1)}), bf16[64,12,768]{2,1,0:T(8,128)(2,1)}, u32[]{:S(2)}, u32[]{:S(2)}) async-start(bf16[64,12,768]{2,1,0:T(8,128)(2,1)} %stack.2), calls=%async_computation | async-start | bytes 3145728 | tf_op jit(solution)/shard_map/all_to_all | solution.py:25
  30.3 551.6 %all-gather.15.cloned.1.call-start = ((), (), s32[]{:S(2)}) async-start(), calls=%async_computation.4 | async-start | bytes 1597440 | tf_op jit(solution)/shard_map/all_gather | solution.py:88
  30.9 848.3 %all-reduce.4.cloned.1.call-start = ((), (), s32[]{:S(2)}) async-start(), calls=%async_computation.5 | async-start | bytes 3145728 | tf_op jit(solution)/shard_map/psum | solution.py:73
  176.8 2.4 copy-start.2
  444.8 2.3 copy-start.3
  585.0 2.7 copy-start.7
  585.0 2.7 copy-start.14
  600.1 2.4 copy-start.5
  600.1 2.4 copy-start.6
  921.4 1.6 copy-start.4
  923.0 1.0 copy-start.1
  924.0 1.0 copy-start.8
  924.0 1.0 copy-start.11
  926.1 2.3 copy-start.9
  926.1 2.3 copy-start.13
Sparse Core Ops, SparseCore 0:
  10.9 152.7 all-gather.10
  166.7 136.4 all-gather.12
  306.1 136.4 all-gather.8
  445.4 136.4 all-gather.14
  603.9 275.1 all-reduce.3
